TPU v7x, 32 devices: a whole 2x2x4 slice. The times are simulated.
32 devices in a mesh: fsdp: 4 (over z), ctx: 2 (over x), tp: 4 (over y, core).
Axes of the slice: x: 2, y: 2, z: 4, core: 2. Of those that a mesh axis runs over, the one named last changes fastest.
Arguments:
- layer_input: bfloat16 [8192, 4096], P(('fsdp', 'ctx'), 'tp'), may hold values from -6 to 6
- attn_gain: bfloat16 [4096], P('tp'), may hold values from 0.099609375 to 1.8984375
- qkv_weight: bfloat16 [4096, 3, 4096], P('fsdp', None, 'tp'), may hold values from -1 to 1
- out_weight: bfloat16 [4096, 4096], P('tp', 'fsdp'), may hold values from -0.75 to 0.75
- ffn_gain: bfloat16 [4096], P('tp'), may hold values from 0.099609375 to 1.8984375
- gate_up_weight: bfloat16 [4096, 2, 11008], P('fsdp', None, 'tp'), may hold values from -0.09375 to 0.09375
- down_weight: bfloat16 [11008, 4096], P('tp', 'fsdp'), may hold values from -0.0546875 to 0.0546875
- cotangent: bfloat16 [8192, 4096], P(('fsdp', 'ctx'), 'tp'), may hold values from -6 to 6
Outputs:
- layer_output: bfloat16 [8192, 4096], P(('fsdp', 'ctx'), 'tp')
- grad_input: float32 [8192, 4096], P(('fsdp', 'ctx'), 'tp')
- grad_attn_gain: float32 [4096], P('tp')
- grad_qkv: float32 [4096, 3, 4096], P(('fsdp', 'ctx'), None, 'tp')
- grad_out_weight: float32 [4096, 4096], P('tp', ('fsdp', 'ctx'))
- grad_ffn_gain: float32 [4096], P('tp')
- grad_gate_up: float32 [4096, 2, 11008], P(('fsdp', 'ctx'), None, 'tp')
- grad_down: float32 [11008, 4096], P('tp', ('fsdp', 'ctx'))
All inputs are finite; a program needn't handle non-finite values.
Results may differ from a plain program's by a relative error of at most 0.018.
Values may be sent and summed in bfloat16 or wider, within the bound.
No kernel may reach another device: no remote copies, remote signals or barrier semaphores. Data moves between devices by JAX's collectives and lax.ppermute only.
A program may use at most 384 MiB of HBM per device.

v0:
```python
import math
import jax
import jax.numpy as jnp
from jax import lax
from jax.sharding import PartitionSpec as P

D = 4096
HD = 128
rms_epsilon = 1e-05
masked_score = -1e30


def rotate(values, positions, direction):
    half_width = HD // 2
    inv_freq = jnp.exp(-math.log(10000.0) * jnp.arange(half_width, dtype=jnp.float32) * 2.0 / HD)
    angles = positions.astype(jnp.float32)[:, None] * inv_freq[None, :]
    cosine = jnp.cos(angles)[:, None, :]
    sine_table = direction * jnp.sin(angles)[:, None, :]
    shaped = values.reshape(values.shape[0], -1, 2, half_width)
    lower_half = shaped[:, :, 0, :]
    upper_half = shaped[:, :, 1, :]
    turned = jnp.stack(
        [
            lower_half * cosine - upper_half * sine_table,
            upper_half * cosine + lower_half * sine_table,
        ],
        axis=2,
    )
    return turned.reshape(values.shape)


def row_total(values):
    return lax.psum(values, "tp")


def full_rows(values):
    return lax.all_gather(values, "tp", axis=1, tiled=True)


def shard_sum(values):
    return lax.psum_scatter(values, "tp", scatter_dimension=1, tiled=True)


def to_heads(values):
    return lax.all_to_all(values, "ctx", split_axis=2, concat_axis=0, tiled=True)


def to_tokens(values):
    return lax.all_to_all(values, "ctx", split_axis=0, concat_axis=2, tiled=True)


def contract_rows(left, right):
    return lax.dot_general(
        left, right, (((0,), (0,)), ((), ())), preferred_element_type=jnp.float32
    )


def contract_cols(left, right):
    return lax.dot_general(
        left, right, (((1,), (1,)), ((), ())), preferred_element_type=jnp.float32
    )


def in_proj(full_input, weight):
    row_count = full_input.shape[0]
    flat_cols = weight.shape[1] * weight.shape[2]
    shard_piece = lax.all_gather(weight, "fsdp", axis=0, tiled=True)
    running = jnp.dot(
        full_input,
        shard_piece.reshape(shard_piece.shape[0], flat_cols),
        preferred_element_type=jnp.float32,
    )
    return running.reshape(row_count, weight.shape[1], weight.shape[2])


def in_proj_back(grads, weight):
    flat_grads = grads.reshape(grads.shape[0], -1)
    shard_piece = lax.all_gather(weight, "fsdp", axis=0, tiled=True)
    return contract_cols(flat_grads, shard_piece.reshape(shard_piece.shape[0], -1))


def out_proj(inner, weight):
    return jnp.dot(
        inner,
        lax.all_gather(weight, "fsdp", axis=1, tiled=True),
        preferred_element_type=jnp.float32,
    )


def out_proj_back(full_grad, weight):
    return contract_cols(full_grad, lax.all_gather(weight, "fsdp", axis=1, tiled=True))


def reduce_grads(first_grad, second_grad):
    reduced = (
        lax.psum_scatter(
            first_grad.astype(jnp.bfloat16), ("fsdp", "ctx"), scatter_dimension=0, tiled=True
        ).astype(jnp.float32),
        lax.psum_scatter(
            second_grad.astype(jnp.bfloat16), ("fsdp", "ctx"), scatter_dimension=0, tiled=True
        ).astype(jnp.float32),
    )
    return reduced


def score_block(query_heads, key_heads, first_row, block_len):
    query_block = lax.dynamic_slice_in_dim(query_heads, first_row, block_len, 0)
    scores = jnp.einsum("qhd,khd->hqk", query_block, key_heads, preferred_element_type=jnp.float32)
    scores = scores * (1.0 / math.sqrt(HD))
    key_index = jnp.arange(key_heads.shape[0], dtype=jnp.int32)
    query_index = first_row + jnp.arange(block_len, dtype=jnp.int32)
    allowed = key_index[None, :] <= query_index[:, None]
    return (query_block, jnp.where(allowed[None, :, :], scores, masked_score))


def attend_forward(qkv_heads):
    seq_len = qkv_heads.shape[0]
    head_count = qkv_heads.shape[2] // HD
    block_len = min(512, seq_len)
    block_count = seq_len // block_len
    query_heads = qkv_heads[:, 0].reshape(seq_len, head_count, HD)
    key_heads = qkv_heads[:, 1].reshape(seq_len, head_count, HD)
    value_heads = qkv_heads[:, 2].reshape(seq_len, head_count, HD)

    def one_block(block_index):
        query_block, scores = score_block(
            query_heads, key_heads, block_index * block_len, block_len
        )
        row_max = jnp.max(scores, axis=-1, keepdims=True)
        expo_vals = jnp.exp(scores - row_max)
        row_sums = jnp.sum(expo_vals, axis=-1, keepdims=True)
        soft = (expo_vals / row_sums).astype(jnp.bfloat16)
        mixed = jnp.einsum("hqk,khd->qhd", soft, value_heads, preferred_element_type=jnp.float32)
        return (mixed.astype(jnp.bfloat16), (row_max + jnp.log(row_sums))[:, :, 0])

    head_outs, log_norms = lax.map(one_block, jnp.arange(block_count, dtype=jnp.int32))
    return (head_outs.reshape(seq_len, 1, head_count * HD), log_norms)


def attend_backward(qkv_heads, log_norms, grad_out):
    seq_len = qkv_heads.shape[0]
    head_count = qkv_heads.shape[2] // HD
    block_len = min(512, seq_len)
    block_count = seq_len // block_len
    score_scale = 1.0 / math.sqrt(HD)
    query_heads = qkv_heads[:, 0].reshape(seq_len, head_count, HD)
    key_heads = qkv_heads[:, 1].reshape(seq_len, head_count, HD)
    value_heads = qkv_heads[:, 2].reshape(seq_len, head_count, HD)
    grad_heads = grad_out.reshape(seq_len, head_count, HD)

    def one_block(running_grads, block_item):
        block_index, block_norms = block_item
        first_row = block_index * block_len
        query_block, scores = score_block(query_heads, key_heads, first_row, block_len)
        probs_full = jnp.exp(scores - block_norms[:, :, None])
        soft = probs_full.astype(jnp.bfloat16)
        grad_block = lax.dynamic_slice_in_dim(grad_heads, first_row, block_len, 0)
        grad_probs = jnp.einsum(
            "qhd,khd->hqk", grad_block, value_heads, preferred_element_type=jnp.float32
        )
        weighted = jnp.sum(probs_full * grad_probs, axis=-1, keepdims=True)
        grad_scores = (probs_full * (grad_probs - weighted)).astype(jnp.bfloat16)
        query_grad = (
            jnp.einsum("hqk,khd->qhd", grad_scores, key_heads, preferred_element_type=jnp.float32)
            * score_scale
        )
        key_grad = (
            running_grads[0]
            + jnp.einsum(
                "hqk,qhd->khd", grad_scores, query_block, preferred_element_type=jnp.float32
            )
            * score_scale
        )
        value_grad = running_grads[1] + jnp.einsum(
            "hqk,qhd->khd", soft, grad_block, preferred_element_type=jnp.float32
        )
        return ((key_grad, value_grad), query_grad)

    zero_grads = jnp.zeros((seq_len, head_count, HD), jnp.float32)
    key_value, query_grads = lax.scan(
        one_block, (zero_grads, zero_grads), (jnp.arange(block_count, dtype=jnp.int32), log_norms)
    )
    flat_width = head_count * HD
    return (
        query_grads.reshape(seq_len, flat_width),
        key_value[0].reshape(seq_len, flat_width),
        key_value[1].reshape(seq_len, flat_width),
    )


def body(
    layer_input, attn_gain, qkv_weight, out_weight, ffn_gain, gate_up_weight, down_weight, cotangent
):
    row_count = layer_input.shape[0]
    input_float = layer_input.astype(jnp.float32)
    attn_scale = attn_gain.astype(jnp.float32)
    ffn_scale = ffn_gain.astype(jnp.float32)
    rms_one = lax.rsqrt(row_total(jnp.sum(input_float * input_float, axis=-1)) / D + rms_epsilon)[
        :, None
    ]
    normed_attn = (input_float * rms_one * attn_scale).astype(jnp.bfloat16)
    attn_full = full_rows(normed_attn)
    proj = in_proj(attn_full, qkv_weight)
    positions = lax.axis_index("ctx") * row_count + jnp.arange(row_count, dtype=jnp.int32)
    qkv_local = jnp.stack(
        [rotate(proj[:, 0], positions, 1.0), rotate(proj[:, 1], positions, 1.0), proj[:, 2]], axis=1
    ).astype(jnp.bfloat16)
    qkv_heads = to_heads(qkv_local)
    seq_len = qkv_heads.shape[0]
    head_outs, log_norms = attend_forward(qkv_heads)
    attn_tokens = to_tokens(head_outs)[:, 0, :]
    resid = input_float + shard_sum(out_proj(attn_tokens, out_weight))
    rms_two = lax.rsqrt(row_total(jnp.sum(resid * resid, axis=-1)) / D + rms_epsilon)[:, None]
    normed_ffn = (resid * rms_two * ffn_scale).astype(jnp.bfloat16)
    ffn_full = full_rows(normed_ffn)
    gate_up = in_proj(ffn_full, gate_up_weight)
    gate = gate_up[:, 0]
    up_value = gate_up[:, 1]
    sigma = jax.nn.sigmoid(gate)
    hidden = (gate * sigma * up_value).astype(jnp.bfloat16)
    layer_output = (resid + shard_sum(out_proj(hidden, down_weight))).astype(jnp.bfloat16)
    cotan_full = full_rows(cotangent)
    grad_hidden = out_proj_back(cotan_full, down_weight)
    down_grad_t = contract_rows(cotan_full, hidden)
    grad_gu = jnp.stack(
        [grad_hidden * up_value * sigma * (1.0 + gate * (1.0 - sigma)), grad_hidden * gate * sigma],
        axis=1,
    ).astype(jnp.bfloat16)
    grad_nffn = shard_sum(in_proj_back(grad_gu, gate_up_weight))
    gate_up_grad = contract_rows(ffn_full, grad_gu.reshape(row_count, -1)).reshape(D, 2, -1)
    ffn_reduced = reduce_grads(gate_up_grad, down_grad_t)
    ffn_term = grad_nffn * ffn_scale
    ffn_dot = row_total(jnp.sum(ffn_term * resid, axis=-1))[:, None]
    grad_resid = (
        cotangent.astype(jnp.float32) + rms_two * ffn_term - resid * rms_two**3 * ffn_dot / D
    )
    ffn_gain_part = jnp.sum(grad_nffn * resid * rms_two, axis=0)
    grad_branch = grad_resid.astype(jnp.bfloat16)
    branch_full = full_rows(grad_branch)
    grad_attn_tokens = out_proj_back(branch_full, out_weight).astype(jnp.bfloat16)
    out_grad_t = contract_rows(branch_full, attn_tokens)
    grad_out_heads = to_heads(grad_attn_tokens[:, None, :])
    query_grad, key_grad, value_grad = attend_backward(qkv_heads, log_norms, grad_out_heads)
    all_positions = jnp.arange(seq_len, dtype=jnp.int32)
    grad_proj_heads = jnp.stack(
        [
            rotate(query_grad, all_positions, -1.0),
            rotate(key_grad, all_positions, -1.0),
            value_grad,
        ],
        axis=1,
    ).astype(jnp.bfloat16)
    grad_proj = to_tokens(grad_proj_heads)
    grad_nattn = shard_sum(in_proj_back(grad_proj, qkv_weight))
    qkv_grad = contract_rows(attn_full, grad_proj.reshape(row_count, -1)).reshape(D, 3, -1)
    attn_reduced = reduce_grads(qkv_grad, out_grad_t)
    attn_term = grad_nattn * attn_scale
    attn_dot = row_total(jnp.sum(attn_term * input_float, axis=-1))[:, None]
    grad_input = grad_resid + rms_one * attn_term - input_float * rms_one**3 * attn_dot / D
    attn_gain_part = jnp.sum(grad_nattn * input_float * rms_one, axis=0)
    gain_grads = lax.psum((attn_gain_part, ffn_gain_part), ("fsdp", "ctx"))
    return (
        layer_output,
        grad_input,
        gain_grads[0],
        attn_reduced[0],
        attn_reduced[1].T,
        gain_grads[1],
        ffn_reduced[0],
        ffn_reduced[1].T,
    )


def solution(mesh):
    return jax.shard_map(
        body,
        mesh=mesh,
        in_specs=(
            P(("fsdp", "ctx"), "tp"),
            P("tp"),
            P("fsdp", None, "tp"),
            P("tp", "fsdp"),
            P("tp"),
            P("fsdp", None, "tp"),
            P("tp", "fsdp"),
            P(("fsdp", "ctx"), "tp"),
        ),
        out_specs=(
            P(("fsdp", "ctx"), "tp"),
            P(("fsdp", "ctx"), "tp"),
            P("tp"),
            P(("fsdp", "ctx"), None, "tp"),
            P("tp", ("fsdp", "ctx")),
            P("tp"),
            P(("fsdp", "ctx"), None, "tp"),
            P("tp", ("fsdp", "ctx")),
        ),
        check_vma=False,
    )
```

profile of v0, /device:TPU:0, one launch (start us, length us, event | category | flops | bytes accessed | tf_op | source)
XLA Modules:
  0.0 4553.2 jit_solution(1638973924265543728)
XLA Ops:
  33.3 48.4 %all-gather.9.cloned.1.call-done = bf16[1024,4096]{1,0:T(8,128)(2,1)} async-done(((bf16[1024,1024]{1,0:T(8,128)(2,1)}), bf16[1024,4096]{1,0:T(8,128)(2,1)}) %all-gather.9.cloned.1.call-update) | async-done | bytes 8388624 | tf_op jit(solution)/shard_map/all_gather | solution.py:37
  81.8 427.4 %all-gather.11.cloned.1.call-done = bf16[4096,3,1024]{0,2,1:T(8,128)(2,1)} async-done(((bf16[1024,3,1024]{0,2,1:T(8,128)(2,1)}), bf16[4096,3,1024]{0,2,1:T(8,128)(2,1)}) %all-gather.11.cloned.1.call-update) | async-done | bytes 25165840 | tf_op jit(solution)/shard_map/all_gather | solution.py:67
  509.1 32.0 fusion.29
  570.5 92.0 %all-to-all-done = bf16[1024,3,1024]{0,1,2:T(4,128)(2,1)} async-done(((bf16[1024,3,1024]{0,1,2:T(4,128)(2,1)}), bf16[1024,3,1024]{0,1,2:T(4,128)(2,1)}, u32[]{:S(2)}, u32[]{:S(2)}) %all-to-all-start) | async-done | bytes 6291488 | tf_op jit(solution)/shard_map/all_to_all | solution.py:45
  706.0 72.8 %while.27 = (s32[]{:T(128)}, bf16[4,512,4,128]{3,2,1,0:T(4,128)(2,1)}, f32[4,4,512]{2,1,0:T(4,128)}, s32[4]{0:T(128)S(1)}, bf16[2048,4,128]{2,0,1:T(8,128)(2,1)}...) while((s32[]{:T(128)}, ...), condition=%wide.region_5.6_spmd, body=%wide.region_2.5_spmd.sunk | while | flops 2199124480 | bytes 69275856 | solution.py:136
  778.8 12.7 reshape.256
  792.1 15.4 reduce
  811.3 28.4 all_to_all.63
  848.0 16.2 fusion.52
  864.9 122.8 %reduce-scatter.9.cloned.1.call-done = f32[1024,1024]{1,0:T(8,128)} async-done(((f32[1024,4096]{1,0:T(8,128)}), f32[1024,1024]{1,0:T(8,128)}) %reduce-scatter.9.cloned.1.call-update) | async-done | bytes 4194320 | tf_op jit(solution)/shard_map/reduce_scatter | solution.py:41
  1006.6 733.5 %all-gather.17.cloned.1.call-done = bf16[4096,2,2752]{0,2,1:T(8,128)(2,1)} async-done(((bf16[1024,2,2752]{0,2,1:T(8,128)(2,1)}), bf16[4096,2,2752]{0,2,1:T(8,128)(2,1)}) %all-gather.17.cloned.1.call-update) | async-done | bytes 45088784 | tf_op jit(solution)/shard_map/all_gather | solution.py:67
  1740.1 58.6 %all-gather.15.cloned.1.call-done = bf16[1024,4096]{1,0:T(8,128)(2,1)} async-done(((bf16[1024,1024]{1,0:T(8,128)(2,1)}), bf16[1024,4096]{1,0:T(8,128)(2,1)}) %all-gather.15.cloned.1.call-update) | async-done | bytes 8388624 | tf_op jit(solution)/shard_map/all_gather | solution.py:37
  1798.7 55.6 %fusion.27 = f32[1024,2,2752]{0,2,1:T(8,128)} fusion(bf16[4096,2,2752]{0,2,1:T(8,128)(2,1)} %all-gather.17.cloned.1.call-done, bf16[1024,4096]{1,0:T(8,128)(2,1)} %all-gather.15.cloned.1.call-done), kind=kOutput, calls=%fused_computation.41 | convolution fusion | flops 46170898432 | bytes 76021760 | tf_op jit(solution)/shard_map/dot_general | solution.py:68
  1858.6 384.2 %all-gather.19.cloned.1.call-done = bf16[2752,4096]{1,0:T(8,128)(2,1)} async-done(((bf16[2752,1024]{1,0:T(8,128)(2,1)}), bf16[2752,4096]{1,0:T(8,128)(2,1)}) %all-gather.19.cloned.1.call-update) | async-done | bytes 22544400 | tf_op jit(solution)/shard_map/all_gather | solution.py:85
  2242.8 37.2 multiply_bitcast_fusion.1
  2280.0 58.4 %convolution_bitcast_fusion = f32[1024,4096]{1,0:T(8,128)} fusion(bf16[4096,2,2752]{0,2,1:T(8,128)(2,1)} %all-gather.17.cloned.1.call-done, bf16[1024,1,2752]{0,2,1:T(8,128)(2,1)} %get-tuple-element.270, bf16[1024,1,2752]{0,2,1:T(8,128)(2,1)} %get-tuple-element.269), kind=kOutput, calls=%fused_computation.63 | convolution fusion | flops 46176534528 | bytes 73138176 | tf_op jit(solution)/shard_map/dot_general | solution.py:59
  2353.5 31.8 fusion.53
  2385.4 77.8 %reduce-scatter.13.cloned.1.call-done = f32[1024,1024]{1,0:T(8,128)} async-done(((f32[1024,4096]{1,0:T(8,128)}), f32[1024,1024]{1,0:T(8,128)}) %reduce-scatter.13.cloned.1.call-update) | async-done | bytes 4194320 | tf_op jit(solution)/shard_map/reduce_scatter | solution.py:41
  2474.0 117.8 %reduce-scatter.11.cloned.1.call-done = f32[1024,1024]{1,0:T(8,128)} async-done(((f32[1024,4096]{1,0:T(8,128)}), f32[1024,1024]{1,0:T(8,128)}) %reduce-scatter.11.cloned.1.call-update) | async-done | bytes 4194320 | tf_op jit(solution)/shard_map/reduce_scatter | solution.py:41
  2599.2 31.3 fusion.31
  2633.9 23.7 all-gather.23.cloned.1.call-done
  2657.6 13.7 convert_bitcast_fusion.2
  2678.9 13.0 reduce.1
  2698.2 15.1 convolution_convert_fusion.3
  2713.4 24.8 all-to-all-done.2
  2753.8 356.8 %while.28 = (s32[]{:T(128)}, f32[2048,4,128]{0,2,1:T(8,128)}, f32[2048,4,128]{0,2,1:T(8,128)}, f32[4,512,4,128]{1,0,3,2:T(4,128)}, s32[4]{0:T(128)S(1)}, /*index...) while((s32[]{:T(128)}, f32[2048,4,128]{0,2,1:T(8,128)}, ...), condition=%wide.region_15.16_spmd.clone, body=%wide.region_13.15_spmd.clone.sunk | while | flops 5438175744 | bytes 199291264 | solution.py:180
  2779.9 15.8 multiply_convert_fusion.4
  2820.3 21.1 dynamic_update_slice.20
  2854.6 12.8 multiply_reduce_fusion.5
  2867.3 15.1 multiply_convert_fusion.4
  2909.7 21.0 dynamic_update_slice.20
  2956.7 15.5 multiply_convert_fusion.4
  2981.1 12.8 bitcast_add_fusion.5
  2999.6 21.1 dynamic_update_slice.20
  3033.8 12.8 multiply_reduce_fusion.5
  3046.6 15.4 multiply_convert_fusion.4
  3070.7 12.8 bitcast_add_fusion.5
  3089.2 21.1 dynamic_update_slice.20
  3127.9 14.1 copy.90
  3142.0 103.0 %all_to_all.64 = bf16[2048,3,512]{2,1,0:T(4,128)(2,1)} all-to-all(bf16[2048,3,512]{2,1,0:T(4,128)(2,1)} %copy.90), channel_id=1, replica_groups=mesh['fsdp'=4,'ctx'=2,'tp'=4] {'ctx'}, dimensions={0} | all-to-all | bytes 12582912 | tf_op jit(solution)/shard_map/all_to_all | solution.py:49
  3245.1 13.0 copy.91
  3258.1 33.8 fusion.54
  3291.9 55.4 %convolution_convert_fusion = bf16[4096,2,2752]{0,2,1:T(8,128)(2,1)} fusion(bf16[1024,4096]{1,0:T(8,128)(2,1)} %all-gather.15.cloned.1.call-done, bf16[1024,1,2752]{0,2,1:T(8,128)(2,1)} %get-tuple-element.270, bf16[1024,1,2752]{0,2,1:T(8,128)(2,1)} %get-tuple-element.269), kind=kOutput, calls=%fused_computation.43 | convolution fusion | flops 46215987200 | bytes 64749568 | tf_op jit(solution)/shard_map/dot_general | solution.py:53
  3347.4 34.6 convolution_convert_fusion.2
  3393.0 25.1 reduce-scatter.15.cloned.1.call-done
  3421.6 22.7 all-reduce
  3456.0 677.8 %reduce-scatter.21.cloned.1.call-done = bf16[512,2,2752]{0,2,1:T(8,128)(2,1)} async-done(((bf16[4096,2,2752]{0,2,1:T(8,128)(2,1)}), bf16[512,2,2752]{0,2,1:T(8,128)(2,1)}) %reduce-scatter.21.cloned.1.call-update) | async-done | bytes 5636112 | tf_op jit(solution)/shard_map/reduce_scatter | solution.py:96
  4142.3 398.8 %reduce-scatter.17.cloned.1.call-done = bf16[512,3,1024]{2,0,1:T(8,128)(2,1)} async-done(((bf16[4096,3,1024]{2,0,1:T(8,128)(2,1)}), bf16[512,3,1024]{2,0,1:T(8,128)(2,1)}) %reduce-scatter.17.cloned.1.call-update) | async-done | bytes 3145744 | tf_op jit(solution)/shard_map/reduce_scatter | solution.py:96
  (275 shorter events, 485.2 us)
Async XLA Ops:
  7.2 74.6 %all-gather.9.cloned.1.call-start = ((), (), s32[]{:S(2)}) async-start(), calls=%async_computation.12 | async-start | bytes 10485760 | tf_op jit(solution)/shard_map/all_gather | solution.py:37
  7.9 15.1 copy-start.19
  23.0 486.1 %all-gather.11.cloned.1.call-start = ((), (), s32[]{:S(2)}) async-start(), calls=%async_computation.13 | async-start | bytes 31457280 | tf_op jit(solution)/shard_map/all_gather | solution.py:67
  562.7 99.9 %all-to-all-start = ((bf16[1024,3,1024]{0,1,2:T(4,128)(2,1)}), bf16[1024,3,1024]{0,1,2:T(4,128)(2,1)}, u32[]{:S(2)}, u32[]{:S(2)}) async-start(bf16[1024,3,1024]{0,1,2:T(4,128)(2,1)} %copy.71), calls=%async_computation | async-start | bytes 16777216 | tf_op jit(solution)/shard_map/all_to_all | solution.py:45
  569.7 278.3 %all-gather.13.cloned.1.call-start = ((), (), s32[]{:S(2)}) async-start(), calls=%async_computation.14 | async-start | bytes 10485760 | tf_op jit(solution)/shard_map/all_gather | solution.py:85
  570.4 417.3 %reduce-scatter.9.cloned.1.call-start = ((), (), s32[]{:S(2)}) async-start(), calls=%async_computation.15 | async-start | bytes 20971520 | tf_op jit(solution)/shard_map/reduce_scatter | solution.py:41
  778.8 28.8 copy-start
  864.3 123.5 %copy-start.6 = (bf16[1024,1024]{1,0:T(8,128)(2,1)S(1)}, bf16[1024,1024]{1,0:T(8,128)(2,1)}, u32[]{:S(2)}) copy-start(bf16[1024,1024]{1,0:T(8,128)(2,1)} %param.12) | copy-start | bytes 6291460
  864.3 875.8 %all-gather.17.cloned.1.call-start = ((), (), s32[]{:S(2)}) async-start(), calls=%async_computation.17 | async-start | bytes 56360960 | tf_op jit(solution)/shard_map/all_gather | solution.py:67
  864.9 933.8 %all-gather.15.cloned.1.call-start = ((), (), s32[]{:S(2)}) async-start(), calls=%async_computation.16 | async-start | bytes 10485760 | tf_op jit(solution)/shard_map/all_gather | solution.py:37
  864.9 133.9 %copy-start.15 = (f32[1024]{0:T(1024)}, f32[1024]{0:T(1024)S(1)}, u32[]{:S(2)}) copy-start(f32[1024]{0:T(1024)S(1)} %convert_element_type.111) | copy-start | bytes 12292
  1005.0 853.6 %all-gather.21.cloned.1.call-start = ((), (), s32[]{:S(2)}) async-start(), calls=%async_computation.20 | async-start | bytes 10485760 | tf_op jit(solution)/shard_map/all_gather | solution.py:37
  1005.8 1237.0 %all-gather.19.cloned.1.call-start = ((), (), s32[]{:S(2)}) async-start(), calls=%async_computation.18 | async-start | bytes 28180480 | tf_op jit(solution)/shard_map/all_gather | solution.py:85
  1006.6 1456.6 %reduce-scatter.13.cloned.1.call-start = ((), (), s32[]{:S(2)}) async-start(), calls=%async_computation.21 | async-start | bytes 20971520 | tf_op jit(solution)/shard_map/reduce_scatter | solution.py:41
  2338.5 253.2 %reduce-scatter.11.cloned.1.call-start = ((), (), s32[]{:S(2)}) async-start(), calls=%async_computation.19 | async-start | bytes 20971520 | tf_op jit(solution)/shard_map/reduce_scatter | solution.py:41
  2385.3 77.9 %copy-start.14 = (f32[1024]{0:T(1024)S(1)}, f32[1024]{0:T(1024)}, u32[]{:S(2)}) copy-start(f32[1024]{0:T(1024)} %copy-done.13) | copy-start | bytes 12292
  2385.3 77.9 %copy-start.16 = (f32[1024]{0:T(1024)S(1)}, f32[1024]{0:T(1024)}, u32[]{:S(2)}) copy-start(f32[1024]{0:T(1024)} %copy-done.15) | copy-start | bytes 12292
  2385.3 206.4 %copy-start.8 = (bf16[1024,1024]{1,0:T(8,128)(2,1)S(1)}, bf16[1024,1024]{1,0:T(8,128)(2,1)}, u32[]{:S(2)}) copy-start(bf16[1024,1024]{1,0:T(8,128)(2,1)} %param.19) | copy-start | bytes 6291460
  2385.3 206.4 %copy-start.22 = (f32[1024]{0:T(1024)S(1)}, f32[1024]{0:T(1024)}, u32[]{:S(2)}) copy-start(f32[1024]{0:T(1024)} %get-tuple-element.295) | copy-start | bytes 12292
  2385.3 272.3 %all-gather.23.cloned.1.call-start = ((), (), s32[]{:S(2)}) async-start(), calls=%async_computation.22 | async-start | bytes 10485760 | tf_op jit(solution)/shard_map/all_gather | solution.py:37
  2599.2 782.9 %reduce-scatter.23.cloned.1.call-start = ((), (), s32[]{:S(2)}) async-start(), calls=%async_computation.27 | async-start | bytes 25362432 | tf_op jit(solution)/shard_map/reduce_scatter | solution.py:99
  2694.4 43.8 all-to-all-start.2
  2698.2 689.0 %reduce-scatter.19.cloned.1.call-start = ((), (), s32[]{:S(2)}) async-start(), calls=%async_computation.25 | async-start | bytes 9437184 | tf_op jit(solution)/shard_map/reduce_scatter | solution.py:99
  2713.3 704.8 %reduce-scatter.15.cloned.1.call-start = ((), (), s32[]{:S(2)}) async-start(), calls=%async_computation.23 | async-start | bytes 20971520 | tf_op jit(solution)/shard_map/reduce_scatter | solution.py:41
  2755.2 12.0 copy-start.3
  2767.3 12.7 copy-start.4
  2795.7 18.9 slice-start
  2803.1 11.5 slice-start.1
  2842.6 11.9 copy-start.3
  2854.5 12.8 copy-start.4
  2882.5 9.1 copy-start.5
  2882.5 21.5 slice-start
  2891.6 12.4 slice-start.1
  2932.0 12.0 copy-start.3
  2944.0 12.6 copy-start.4
  2972.1 21.7 slice-start
  2981.1 12.8 slice-start.1
  3021.9 11.9 copy-start.3
  3033.7 12.8 copy-start.4
  3061.9 21.5 slice-start
  3070.7 12.8 slice-start.1
  3291.8 841.9 %reduce-scatter.21.cloned.1.call-start = ((), (), s32[]{:S(2)}) async-start(), calls=%async_computation.26 | async-start | bytes 50724864 | tf_op jit(solution)/shard_map/reduce_scatter | solution.py:96
  3347.3 1193.8 %reduce-scatter.17.cloned.1.call-start = ((), (), s32[]{:S(2)}) async-start(), calls=%async_computation.24 | async-start | bytes 28311552 | tf_op jit(solution)/shard_map/reduce_scatter | solution.py:96
  3387.1 31.0 copy-start.7
  3387.1 31.0 copy-start.18
  3387.1 31.0 copy-start.20
  3393.0 28.6 copy-start.23
  3393.0 57.4 %copy-start.21 = (f32[1024]{0:T(1024)S(1)}, f32[1024]{0:T(1024)}, u32[]{:S(2)}) copy-start(f32[1024]{0:T(1024)} %get-tuple-element.293) | copy-start | bytes 12292
  (17 other events, 71.1 us)
Sparse Core Ops, SparseCore 0:
  23.1 58.5 all-gather.8
  83.9 425.1 all-gather.10
  572.1 148.3 all-gather.12
  864.4 123.3 reduce-scatter.8
  989.3 750.7 all-gather.16
  1742.2 56.4 all-gather.14
  1800.3 58.2 all-gather.20
  1860.3 382.5 all-gather.18
  2338.6 124.4 reduce-scatter.12
  2465.6 126.1 reduce-scatter.10
  2599.3 58.2 all-gather.22
  2662.0 366.1 reduce-scatter.22
  3031.8 148.1 reduce-scatter.18
  3292.0 126.0 reduce-scatter.14
  3421.9 711.7 reduce-scatter.20
  4137.5 403.5 reduce-scatter.16
where the time goes:
time: 4570 us; the launch traced here: 4550 us
  waiting for transfers between devices  3220 us (70%)
  matrix products  640 us (14%)
  local copies, waits for them, and re-layouts  272 us (6%)
  other arithmetic  209 us (5%)
  blocking collectives  180 us (4%)
    all_gather x2, waiting for transfers between devices, in_proj(): shard_piece = lax.all_gather(weight, 'fsdp', axis=0, tiled=True)  1160 us
    reduce_scatter x2, waiting for transfers between devices, reduce_grads(): lax.psum_scatter(first_grad.astype(jnp.bfloat16), ('fsdp', 'ctx'), scatte...  1080 us
    all_gather x2, waiting for transfers between devices, out_proj(): lax.all_gather(weight, 'fsdp', axis=1, tiled=True)  384 us
    reduce_scatter x4, waiting for transfers between devices, shard_sum(): return lax.psum_scatter(values, 'tp', scatter_dimension=1, tiled=True)  343 us
    dot_general x4, matrix products, contract_cols(): lax.dot_general(left, right, (((1,), (1,)), ((), ())), preferred_element_...  143 us
    dot_general x4, matrix products, contract_rows(): lax.dot_general(left, right, (((0,), (0,)), ((), ())), preferred_element_...  136 us
    all_gather x4, waiting for transfers between devices, full_rows(): return lax.all_gather(values, 'tp', axis=1, tiled=True)  135 us
    all_to_all x2, blocking collectives, to_tokens(): lax.all_to_all(values, 'ctx', split_axis=0, concat_axis=2, tiled=True)  131 us
  transfers between devices with their start and end apart: 18, of which 15 were waited for; matrix products, arithmetic and copies ran while one was open for 20% of the time, Pallas kernels for 0%

commit v1 on v0

--- a/solution.py
+++ b/solution.py
@@ -62,9 +62,26 @@
 
 
 def in_proj(full_input, weight):
+
+    def map_the_trails(tile_in):
+        devs = lax.axis_size("fsdp")
+        arrivals = [(hop_no, (hop_no + 1) % devs) for hop_no in range(devs)]
+
+        def _see_roots(q_next):
+            if len(q_next) == devs:
+                return q_next
+            f_now = lax.ppermute(q_next[0], axis_name="fsdp", perm=arrivals)
+            before = _see_roots([f_now, *q_next])
+            return before
+
+        v1 = _see_roots([tile_in])
+        oldest = jnp.concatenate(v1, axis=0)
+        r1 = jnp.roll(oldest, shift=(lax.axis_index("fsdp") + 1) * tile_in.shape[0], axis=0)
+        return r1
+
     row_count = full_input.shape[0]
     flat_cols = weight.shape[1] * weight.shape[2]
-    shard_piece = lax.all_gather(weight, "fsdp", axis=0, tiled=True)
+    shard_piece = map_the_trails(weight)
     running = jnp.dot(
         full_input,
         shard_piece.reshape(shard_piece.shape[0], flat_cols),

time: 4570 us -> 5440 us (1.19)
  waiting for transfers between devices: 3220 us -> 3760 us
  starting transfers between devices: 11.5 us -> 219 us
  local copies, waits for them, and re-layouts: 272 us -> 382 us
    ppermute x0 -> x6, waiting for transfers between devices: none -> 1690 us  [_see_roots(): f_now = lax.ppermute(q_next[0], axis_name='fsdp', perm=arrivals)]
    all_gather x2, waiting for transfers between devices: 1160 us -> 183 us  [in_proj_back(): shard_piece = lax.all_gather(weight, 'fsdp', axis=0, tiled=True)]
    all_gather x2, waiting for transfers between devices: 384 us -> 0.01 us  [out_proj(): lax.all_gather(weight, 'fsdp', axis=1, tiled=True)]
    ppermute x0 -> x6, starting transfers between devices: none -> 207 us  [_see_roots(): f_now = lax.ppermute(q_next[0], axis_name='fsdp', perm=arrivals)]
    reduce_scatter x4, waiting for transfers between devices: 343 us -> 527 us  [shard_sum(): return lax.psum_scatter(values, 'tp', scatter_dimension=1, tiled=True)]
    reduce_scatter x2, waiting for transfers between devices: 0.03 us -> 160 us  [reduce_grads(): lax.psum_scatter(second_grad.astype(jnp.bfloat16), ('fsdp', 'ctx'), scatt...]
    all_gather x4, waiting for transfers between devices: 135 us -> 23.2 us  [full_rows(): return lax.all_gather(values, 'tp', axis=1, tiled=True)]
    unnamed x54 -> x84, local copies, waits for them, and re-layouts: 38.1 us -> 122 us
  transfers between devices with their start and end apart: 18 -> 24, of which waited for: 15 -> 18; matrix products, arithmetic and copies ran while one was open for 20% -> 19% of each run, Pallas kernels for 0% -> 0%
where the time goes in v1:
time: 5440 us; the launch traced here: 5420 us
  waiting for transfers between devices  3760 us (69%)
  matrix products  636 us (12%)
  local copies, waits for them, and re-layouts  382 us (7%)
  starting transfers between devices  219 us (4%)
  blocking collectives  216 us (4%)
  other arithmetic  186 us (3%)
    ppermute x6, waiting for transfers between devices, _see_roots(): f_now = lax.ppermute(q_next[0], axis_name='fsdp', perm=arrivals)  1690 us
    reduce_scatter x2, waiting for transfers between devices, reduce_grads(): lax.psum_scatter(first_grad.astype(jnp.bfloat16), ('fsdp', 'ctx'), scatte...  1070 us
    reduce_scatter x4, waiting for transfers between devices, shard_sum(): return lax.psum_scatter(values, 'tp', scatter_dimension=1, tiled=True)  527 us
    ppermute x6, starting transfers between devices, _see_roots(): f_now = lax.ppermute(q_next[0], axis_name='fsdp', perm=arrivals)  207 us
    all_gather x2, waiting for transfers between devices, in_proj_back(): shard_piece = lax.all_gather(weight, 'fsdp', axis=0, tiled=True)  183 us
    all_to_all x2, blocking collectives, to_tokens(): lax.all_to_all(values, 'ctx', split_axis=0, concat_axis=2, tiled=True)  170 us
    reduce_scatter x2, waiting for transfers between devices, reduce_grads(): lax.psum_scatter(second_grad.astype(jnp.bfloat16), ('fsdp', 'ctx'), scatt...  160 us
    dot_general x4, matrix products, contract_cols(): lax.dot_general(left, right, (((1,), (1,)), ((), ())), preferred_element_...  144 us
  transfers between devices with their start and end apart: 24, of which 18 were waited for; matrix products, arithmetic and copies ran while one was open for 19% of the time, Pallas kernels for 0%

profile of v1, /device:TPU:0, one launch (start us, length us, event | category | flops | bytes accessed | tf_op | source)
XLA Modules:
  0.0 5422.7 jit_solution(17436073642055859896)
XLA Ops:
  19.9 137.8 %collective-permute-done = bf16[1024,3,1024]{0,2,1:T(8,128)(2,1)} collective-permute-done((bf16[1024,3,1024]{0,2,1:T(8,128)(2,1)}, bf16[1024,3,1024]{0,2,1:T(8,128)(2,1)}, u32[]{:S(2)}, u32[]{:S(2)}) %collective-permute-start) | collective-permute-done | bytes 6291488 | tf_op jit(solution)/shard_map/ppermute | solution.py:73
  167.1 129.4 %collective-permute-done.1 = bf16[1024,3,1024]{0,2,1:T(8,128)(2,1)} collective-permute-done((bf16[1024,3,1024]{0,2,1:T(8,128)(2,1)}, bf16[1024,3,1024]{0,2,1:T(8,128)(2,1)}, u32[]{:S(2)}, u32[]{:S(2)}) %collective-permute-start.1) | collective-permute-done | bytes 6291488 | tf_op jit(solution)/shard_map/ppermute | solution.py:73
  297.6 136.8 %collective-permute-done.2 = bf16[1024,3,1024]{0,2,1:T(8,128)(2,1)} collective-permute-done((bf16[1024,3,1024]{0,2,1:T(8,128)(2,1)}, bf16[1024,3,1024]{0,2,1:T(8,128)(2,1)}, u32[]{:S(2)}, u32[]{:S(2)}) %collective-permute-start.2) | collective-permute-done | bytes 6291488 | tf_op jit(solution)/shard_map/ppermute | solution.py:73
  477.9 32.3 fusion.30
  536.6 89.6 %all-to-all-done = bf16[1024,3,1024]{0,1,2:T(4,128)(2,1)} async-done(((bf16[1024,3,1024]{0,1,2:T(4,128)(2,1)}), bf16[1024,3,1024]{0,1,2:T(4,128)(2,1)}, u32[]{:S(2)}, u32[]{:S(2)}) %all-to-all-start) | async-done | bytes 6291488 | tf_op jit(solution)/shard_map/all_to_all | solution.py:45
  670.0 72.7 %while.27 = (s32[]{:T(128)}, bf16[4,512,4,128]{3,2,1,0:T(4,128)(2,1)}, f32[4,4,512]{2,1,0:T(4,128)}, s32[4]{0:T(128)S(1)}, bf16[2048,4,128]{2,0,1:T(8,128)(2,1)}...) while((s32[]{:T(128)}, ...), condition=%wide.region_5.6_spmd, body=%wide.region_2.5_spmd.sunk | while | flops 2199124480 | bytes 69276872 | solution.py:153
  742.7 12.7 reshape.259
  755.9 15.3 reduce
  775.0 25.8 all_to_all.63
  809.0 16.2 fusion.56
  825.9 121.9 %reduce-scatter.9.cloned.1.call-done = f32[1024,1024]{1,0:T(8,128)} async-done(((f32[1024,4096]{1,0:T(8,128)}), f32[1024,1024]{1,0:T(8,128)}) %reduce-scatter.9.cloned.1.call-update) | async-done | bytes 4194320 | tf_op jit(solution)/shard_map/reduce_scatter | solution.py:41
  966.9 352.8 %collective-permute-done.3 = bf16[1024,2,2752]{0,2,1:T(8,128)(2,1)S(1)} collective-permute-done((bf16[1024,2,2752]{0,2,1:T(8,128)(2,1)}, bf16[1024,2,2752]{0,2,1:T(8,128)(2,1)S(1)}, u32[]{:S(2)}, u32[]{:S(2)}) %collective-permute-start.3) | collective-permute-done | bytes 11272224 | tf_op jit(solution)/shard_map/ppermute | solution.py:73
  1319.8 114.3 %collective-permute-start.4 = (bf16[1024,2,2752]{0,2,1:T(8,128)(2,1)S(1)}, bf16[1024,2,2752]{0,2,1:T(8,128)(2,1)S(1)}, u32[]{:S(2)}, u32[]{:S(2)}) collective-permute-start(bf16[1024,2,2752]{0,2,1:T(8,128)(2,1)S(1)} %collective-permute-done.3), channel_id=1, source_target_pairs={{0,8},{8,16},{16,24},{24,0},{1,9},{9,17},{17,25},{25,1},{2,10},{10... | collective-permute-start | bytes 33816584 | tf_op jit(solution)/shard_map/ppermute | solution.py:73
  1434.0 452.3 %collective-permute-done.4 = bf16[1024,2,2752]{0,2,1:T(8,128)(2,1)S(1)} collective-permute-done((bf16[1024,2,2752]{0,2,1:T(8,128)(2,1)S(1)}, bf16[1024,2,2752]{0,2,1:T(8,128)(2,1)S(1)}, u32[]{:S(2)}, u32[]{:S(2)}) %collective-permute-start.4) | collective-permute-done | bytes 11272224 | tf_op jit(solution)/shard_map/ppermute | solution.py:73
  1886.4 88.4 %collective-permute-start.5 = (bf16[1024,2,2752]{0,2,1:T(8,128)(2,1)S(1)}, bf16[1024,2,2752]{0,2,1:T(8,128)(2,1)S(1)}, u32[]{:S(2)}, u32[]{:S(2)}) collective-permute-start(bf16[1024,2,2752]{0,2,1:T(8,128)(2,1)S(1)} %collective-permute-done.4), channel_id=1, source_target_pairs={{0,8},{8,16},{16,24},{24,0},{1,9},{9,17},{17,25},{25,1},{2,10},{10... | collective-permute-start | bytes 33816584 | tf_op jit(solution)/shard_map/ppermute | solution.py:73
  1974.7 482.1 %collective-permute-done.5 = bf16[1024,2,2752]{0,2,1:T(8,128)(2,1)S(1)} collective-permute-done((bf16[1024,2,2752]{0,2,1:T(8,128)(2,1)S(1)}, bf16[1024,2,2752]{0,2,1:T(8,128)(2,1)S(1)}, u32[]{:S(2)}, u32[]{:S(2)}) %collective-permute-start.5) | collective-permute-done | bytes 11272224 | tf_op jit(solution)/shard_map/ppermute | solution.py:73
  2506.9 55.3 %fusion.27 = f32[1024,2,2752]{0,2,1:T(8,128)} fusion(bf16[8192,2,2752]{0,2,1:T(8,128)(2,1)} %constant_dynamic-update-slice_fusion.8, s32[]{:T(128)S(6)} %select_n.34, bf16[1024,4096]{1,0:T(8,128)(2,1)} %all-gather.13.cloned.1.call-done), kind=kOutput, calls=%fused_computation.41 | convolution fusion | flops 46170898432 | bytes 76021760 | tf_op jit(solution)/shard_map/dot_general | solution.py:85
  2562.2 37.2 multiply_bitcast_fusion.1
  2599.4 182.8 %all-gather.19.cloned.1.call-done = bf16[4096,2,2752]{0,2,1:T(8,128)(2,1)} async-done(((bf16[1024,2,2752]{0,2,1:T(8,128)(2,1)}), bf16[4096,2,2752]{0,2,1:T(8,128)(2,1)}) %all-gather.19.cloned.1.call-update) | async-done | bytes 45088784 | tf_op jit(solution)/shard_map/all_gather | solution.py:95
  2782.2 58.8 %convolution_bitcast_fusion = f32[1024,4096]{1,0:T(8,128)} fusion(bf16[4096,2,2752]{0,2,1:T(8,128)(2,1)} %all-gather.19.cloned.1.call-done, bf16[1024,1,2752]{0,2,1:T(8,128)(2,1)} %get-tuple-element.270, bf16[1024,1,2752]{0,2,1:T(8,128)(2,1)} %get-tuple-element.269), kind=kOutput, calls=%fused_computation.65 | convolution fusion | flops 46176534528 | bytes 73138176 | tf_op jit(solution)/shard_map/dot_general | solution.py:59
  2852.8 30.3 fusion.57
  2883.2 164.6 %reduce-scatter.13.cloned.1.call-done = f32[1024,1024]{1,0:T(8,128)} async-done(((f32[1024,4096]{1,0:T(8,128)}), f32[1024,1024]{1,0:T(8,128)}) %reduce-scatter.13.cloned.1.call-update) | async-done | bytes 4194320 | tf_op jit(solution)/shard_map/reduce_scatter | solution.py:41
  3058.7 117.9 %reduce-scatter.11.cloned.1.call-done = f32[1024,1024]{1,0:T(8,128)} async-done(((f32[1024,4096]{1,0:T(8,128)}), f32[1024,1024]{1,0:T(8,128)}) %reduce-scatter.11.cloned.1.call-update) | async-done | bytes 4194320 | tf_op jit(solution)/shard_map/reduce_scatter | solution.py:41
  3184.6 31.2 fusion.33
  3219.3 23.2 all-gather.21.cloned.1.call-done
  3242.4 13.8 convert_bitcast_fusion.2
  3263.8 13.2 reduce.1
  3283.3 14.9 convolution_convert_fusion.3
  3324.4 358.3 %while.28 = (s32[]{:T(128)}, f32[2048,4,128]{0,2,1:T(8,128)}, f32[2048,4,128]{0,2,1:T(8,128)}, f32[4,512,4,128]{1,0,3,2:T(4,128)}, s32[4]{0:T(128)S(1)}, /*index...) while((s32[]{:T(128)}, f32[2048,4,128]{0,2,1:T(8,128)}, ...), condition=%wide.region_15.16_spmd.clone, body=%wide.region_13.15_spmd.clone.sunk | while | flops 5438175744 | bytes 207679808 | solution.py:197
  3337.7 12.4 multiply_reduce_fusion.5
  3372.7 21.1 dynamic_update_slice.20
  3425.4 12.4 multiply_reduce_fusion.5
  3460.5 21.1 dynamic_update_slice.20
  3515.6 12.4 multiply_reduce_fusion.5
  3550.7 21.1 dynamic_update_slice.20
  3640.7 21.1 dynamic_update_slice.20
  3699.5 14.1 copy.98
  3713.6 144.5 %all_to_all.64 = bf16[2048,3,512]{2,1,0:T(4,128)(2,1)} all-to-all(bf16[2048,3,512]{2,1,0:T(4,128)(2,1)} %copy.98), channel_id=1, replica_groups=mesh['fsdp'=4,'ctx'=2,'tp'=4] {'ctx'}, dimensions={0} | all-to-all | bytes 12582912 | tf_op jit(solution)/shard_map/all_to_all | solution.py:49
  3858.1 13.1 copy.99
  3871.2 33.8 fusion.58
  3905.0 55.9 %convolution_convert_fusion = bf16[4096,2,2752]{0,2,1:T(8,128)(2,1)} fusion(bf16[1024,4096]{1,0:T(8,128)(2,1)} %all-gather.13.cloned.1.call-done, bf16[1024,1,2752]{0,2,1:T(8,128)(2,1)} %get-tuple-element.270, bf16[1024,1,2752]{0,2,1:T(8,128)(2,1)} %get-tuple-element.269), kind=kOutput, calls=%fused_computation.44 | convolution fusion | flops 46215987200 | bytes 64749568 | tf_op jit(solution)/shard_map/dot_general | solution.py:53
  3961.0 34.7 convolution_convert_fusion.2
  3995.7 15.5 reduce-scatter.23.cloned.1.call-done
  4016.2 144.6 %reduce-scatter.19.cloned.1.call-done = bf16[512,1024]{1,0:T(8,128)(2,1)} async-done(((bf16[4096,1024]{1,0:T(8,128)(2,1)}), bf16[512,1024]{1,0:T(8,128)(2,1)}) %reduce-scatter.19.cloned.1.call-update) | async-done | bytes 1048592 | tf_op jit(solution)/shard_map/reduce_scatter | solution.py:116
  4166.5 122.3 %reduce-scatter.15.cloned.1.call-done = f32[1024,1024]{1,0:T(8,128)} async-done(((f32[1024,4096]{1,0:T(8,128)}), f32[1024,1024]{1,0:T(8,128)}) %reduce-scatter.15.cloned.1.call-update) | async-done | bytes 4194320 | tf_op jit(solution)/shard_map/reduce_scatter | solution.py:41
  4292.3 22.8 all-reduce
  4326.7 676.2 %reduce-scatter.21.cloned.1.call-done = bf16[512,2,2752]{0,2,1:T(8,128)(2,1)} async-done(((bf16[4096,2,2752]{0,2,1:T(8,128)(2,1)}), bf16[512,2,2752]{0,2,1:T(8,128)(2,1)}) %reduce-scatter.21.cloned.1.call-update) | async-done | bytes 5636112 | tf_op jit(solution)/shard_map/reduce_scatter | solution.py:113
  5011.4 398.3 %reduce-scatter.17.cloned.1.call-done = bf16[512,3,1024]{2,0,1:T(8,128)(2,1)} async-done(((bf16[4096,3,1024]{2,0,1:T(8,128)(2,1)}), bf16[512,3,1024]{2,0,1:T(8,128)(2,1)}) %reduce-scatter.17.cloned.1.call-update) | async-done | bytes 3145744 | tf_op jit(solution)/shard_map/reduce_scatter | solution.py:113
  (309 shorter events, 652.2 us)
Async XLA Ops:
  8.0 469.9 %all-gather.9.cloned.1.call-start = ((), (), s32[]{:S(2)}) async-start(), calls=%async_computation.12 | async-start | bytes 10485760 | tf_op jit(solution)/shard_map/all_gather | solution.py:37
  8.0 149.7 %copy-start.29 = (bf16[1024]{0:T(1024)(128)(2,1)S(1)}, bf16[1024]{0:T(1024)(128)(2,1)}, u32[]{:S(2)}) copy-start(bf16[1024]{0:T(1024)(128)(2,1)} %param.13) | copy-start | bytes 6148
  8.1 149.7 %copy-start.8 = (bf16[1024,1024]{1,0:T(8,128)(2,1)S(1)}, bf16[1024,1024]{1,0:T(8,128)(2,1)}, u32[]{:S(2)}) copy-start(bf16[1024,1024]{1,0:T(8,128)(2,1)} %param.12) | copy-start | bytes 6291460
  16.8 140.9 %collective-permute-start = (bf16[1024,3,1024]{0,2,1:T(8,128)(2,1)}, bf16[1024,3,1024]{0,2,1:T(8,128)(2,1)}, u32[]{:S(2)}, u32[]{:S(2)}) collective-permute-start(bf16[1024,3,1024]{0,2,1:T(8,128)(2,1)} %copy.76), channel_id=1, source_target_pairs={{0,8},{8,16},{16,24},{24,0},{1,9},{9,17},{17,25},{25,1},{2,10},{10... | collective-permute-start | bytes 18874376 | tf_op jit(solution)/shard_map/ppermute | solution.py:73
  157.7 138.8 %collective-permute-start.1 = (bf16[1024,3,1024]{0,2,1:T(8,128)(2,1)}, bf16[1024,3,1024]{0,2,1:T(8,128)(2,1)}, u32[]{:S(2)}, u32[]{:S(2)}) collective-permute-start(bf16[1024,3,1024]{0,2,1:T(8,128)(2,1)} %collective-permute-done), channel_id=1, source_target_pairs={{0,8},{8,16},{16,24},{24,0},{1,9},{9,17},{17,25},{25,1},{2,10},{10... | collective-permute-start | bytes 18874376 | tf_op jit(solution)/shard_map/ppermute | solution.py:73
  157.7 138.8 %copy-start.22 = (f32[1024]{0:T(1024)}, f32[1024]{0:T(1024)S(1)}, u32[]{:S(2)}) copy-start(f32[1024]{0:T(1024)S(1)} %convert_element_type.108) | copy-start | bytes 12292
  296.5 137.9 %collective-permute-start.2 = (bf16[1024,3,1024]{0,2,1:T(8,128)(2,1)}, bf16[1024,3,1024]{0,2,1:T(8,128)(2,1)}, u32[]{:S(2)}, u32[]{:S(2)}) collective-permute-start(bf16[1024,3,1024]{0,2,1:T(8,128)(2,1)} %collective-permute-done.1), channel_id=1, source_target_pairs={{0,8},{8,16},{16,24},{24,0},{1,9},{9,17},{17,25},{25,1},{2,10},{10... | collective-permute-start | bytes 18874376 | tf_op jit(solution)/shard_map/ppermute | solution.py:73
  434.4 18.7 slice-start.3
  440.7 12.4 slice-start.4
  529.0 97.2 %all-to-all-start = ((bf16[1024,3,1024]{0,1,2:T(4,128)(2,1)}), bf16[1024,3,1024]{0,1,2:T(4,128)(2,1)}, u32[]{:S(2)}, u32[]{:S(2)}) async-start(bf16[1024,3,1024]{0,1,2:T(4,128)(2,1)} %copy.79), calls=%async_computation | async-start | bytes 16777216 | tf_op jit(solution)/shard_map/all_to_all | solution.py:45
  536.0 273.1 %all-gather.11.cloned.1.call-start = ((), (), s32[]{:S(2)}) async-start(), calls=%async_computation.13 | async-start | bytes 10485760 | tf_op jit(solution)/shard_map/all_gather | solution.py:102
  536.6 411.3 %reduce-scatter.9.cloned.1.call-start = ((), (), s32[]{:S(2)}) async-start(), calls=%async_computation.14 | async-start | bytes 20971520 | tf_op jit(solution)/shard_map/reduce_scatter | solution.py:41
  742.7 28.5 copy-start.1
  825.2 122.6 %copy-start.9 = (bf16[1024,1024]{1,0:T(8,128)(2,1)S(1)}, bf16[1024,1024]{1,0:T(8,128)(2,1)}, u32[]{:S(2)}) copy-start(bf16[1024,1024]{1,0:T(8,128)(2,1)} %param.12) | copy-start | bytes 6291460
  825.2 1681.7 %all-gather.13.cloned.1.call-start = ((), (), s32[]{:S(2)}) async-start(), calls=%async_computation.15 | async-start | bytes 10485760 | tf_op jit(solution)/shard_map/all_gather | solution.py:37
  825.9 137.5 %copy-start.18 = (f32[1024]{0:T(1024)}, f32[1024]{0:T(1024)S(1)}, u32[]{:S(2)}) copy-start(f32[1024]{0:T(1024)S(1)} %convert_element_type.111) | copy-start | bytes 12292
  963.4 1598.8 %all-gather.17.cloned.1.call-start = ((), (), s32[]{:S(2)}) async-start(), calls=%async_computation.18 | async-start | bytes 10485760 | tf_op jit(solution)/shard_map/all_gather | solution.py:37
  964.0 1598.2 %all-gather.15.cloned.1.call-start = ((), (), s32[]{:S(2)}) async-start(), calls=%async_computation.16 | async-start | bytes 28180480 | tf_op jit(solution)/shard_map/all_gather | solution.py:102
  964.6 1817.6 %all-gather.19.cloned.1.call-start = ((), (), s32[]{:S(2)}) async-start(), calls=%async_computation.19 | async-start | bytes 56360960 | tf_op jit(solution)/shard_map/all_gather | solution.py:95
  965.2 2082.7 %reduce-scatter.13.cloned.1.call-start = ((), (), s32[]{:S(2)}) async-start(), calls=%async_computation.20 | async-start | bytes 20971520 | tf_op jit(solution)/shard_map/reduce_scatter | solution.py:41
  965.2 354.5 %collective-permute-start.3 = (bf16[1024,2,2752]{0,2,1:T(8,128)(2,1)}, bf16[1024,2,2752]{0,2,1:T(8,128)(2,1)S(1)}, u32[]{:S(2)}, u32[]{:S(2)}) collective-permute-start(bf16[1024,2,2752]{0,2,1:T(8,128)(2,1)} %param.17), channel_id=1, source_target_pairs={{0,8},{8,16},{16,24},{24,0},{1,9},{9,17},{17,25},{25,1},{2,10},{10... | collective-permute-start | bytes 33816584 | tf_op jit(solution)/shard_map/ppermute | solution.py:73
  1319.8 566.6 %collective-permute-start.4 = (bf16[1024,2,2752]{0,2,1:T(8,128)(2,1)S(1)}, bf16[1024,2,2752]{0,2,1:T(8,128)(2,1)S(1)}, u32[]{:S(2)}, u32[]{:S(2)}) collective-permute-start(bf16[1024,2,2752]{0,2,1:T(8,128)(2,1)S(1)} %collective-permute-done.3), channel_id=1, source_target_pairs={{0,8},{8,16},{16,24},{24,0},{1,9},{9,17},{17,25},{25,1},{2,10},{10... | collective-permute-start | bytes 33816584 | tf_op jit(solution)/shard_map/ppermute | solution.py:73
  1886.4 570.4 %collective-permute-start.5 = (bf16[1024,2,2752]{0,2,1:T(8,128)(2,1)S(1)}, bf16[1024,2,2752]{0,2,1:T(8,128)(2,1)S(1)}, u32[]{:S(2)}, u32[]{:S(2)}) collective-permute-start(bf16[1024,2,2752]{0,2,1:T(8,128)(2,1)S(1)} %collective-permute-done.4), channel_id=1, source_target_pairs={{0,8},{8,16},{16,24},{24,0},{1,9},{9,17},{17,25},{25,1},{2,10},{10... | collective-permute-start | bytes 33816584 | tf_op jit(solution)/shard_map/ppermute | solution.py:73
  2841.0 335.6 %reduce-scatter.11.cloned.1.call-start = ((), (), s32[]{:S(2)}) async-start(), calls=%async_computation.17 | async-start | bytes 20971520 | tf_op jit(solution)/shard_map/reduce_scatter | solution.py:41
  2883.1 164.7 %copy-start.17 = (f32[1024]{0:T(1024)S(1)}, f32[1024]{0:T(1024)}, u32[]{:S(2)}) copy-start(f32[1024]{0:T(1024)} %copy-done.16) | copy-start | bytes 12292
  2883.1 164.7 %copy-start.19 = (f32[1024]{0:T(1024)S(1)}, f32[1024]{0:T(1024)}, u32[]{:S(2)}) copy-start(f32[1024]{0:T(1024)} %copy-done.18) | copy-start | bytes 12292
  2883.1 293.5 %copy-start.12 = (bf16[1024,1024]{1,0:T(8,128)(2,1)S(1)}, bf16[1024,1024]{1,0:T(8,128)(2,1)}, u32[]{:S(2)}) copy-start(bf16[1024,1024]{1,0:T(8,128)(2,1)} %param.19) | copy-start | bytes 6291460
  2883.1 293.4 %copy-start.25 = (f32[1024]{0:T(1024)S(1)}, f32[1024]{0:T(1024)}, u32[]{:S(2)}) copy-start(f32[1024]{0:T(1024)} %get-tuple-element.295) | copy-start | bytes 12292
  2883.1 359.3 %all-gather.21.cloned.1.call-start = ((), (), s32[]{:S(2)}) async-start(), calls=%async_computation.21 | async-start | bytes 10485760 | tf_op jit(solution)/shard_map/all_gather | solution.py:37
  3184.0 687.2 %all-gather.23.cloned.1.call-start = ((), (), s32[]{:S(2)}) async-start(), calls=%async_computation.22 | async-start | bytes 31457280 | tf_op jit(solution)/shard_map/all_gather | solution.py:95
  3184.6 826.6 %reduce-scatter.23.cloned.1.call-start = ((), (), s32[]{:S(2)}) async-start(), calls=%async_computation.27 | async-start | bytes 25362432 | tf_op jit(solution)/shard_map/reduce_scatter | solution.py:116
  3279.5 29.4 all-to-all-start.2
  3283.3 877.6 %reduce-scatter.19.cloned.1.call-start = ((), (), s32[]{:S(2)}) async-start(), calls=%async_computation.25 | async-start | bytes 9437184 | tf_op jit(solution)/shard_map/reduce_scatter | solution.py:116
  3298.3 990.5 %reduce-scatter.15.cloned.1.call-start = ((), (), s32[]{:S(2)}) async-start(), calls=%async_computation.23 | async-start | bytes 20971520 | tf_op jit(solution)/shard_map/reduce_scatter | solution.py:41
  3312.0 12.4 copy-start.2
  3336.3 13.8 copy-start.6
  3413.5 11.9 copy-start.5
  3424.0 13.8 copy-start.6
  3503.7 11.9 copy-start.5
  3514.2 13.8 copy-start.6
  3604.4 13.8 copy-start.6
  3905.0 1097.9 %reduce-scatter.21.cloned.1.call-start = ((), (), s32[]{:S(2)}) async-start(), calls=%async_computation.26 | async-start | bytes 50724864 | tf_op jit(solution)/shard_map/reduce_scatter | solution.py:113
  3960.9 1448.8 %reduce-scatter.17.cloned.1.call-start = ((), (), s32[]{:S(2)}) async-start(), calls=%async_computation.24 | async-start | bytes 28311552 | tf_op jit(solution)/shard_map/reduce_scatter | solution.py:113
  3995.6 293.2 %copy-start.10 = (bf16[1024,1024]{1,0:T(8,128)(2,1)S(1)}, bf16[1024,1024]{1,0:T(8,128)(2,1)}, u32[]{:S(2)}) copy-start(bf16[1024,1024]{1,0:T(8,128)(2,1)} %param.12) | copy-start | bytes 6291460
  3995.6 293.2 %copy-start.21 = (f32[1024]{0:T(1024)S(1)}, f32[1024]{0:T(1024)}, u32[]{:S(2)}) copy-start(f32[1024]{0:T(1024)} %copy-done.20) | copy-start | bytes 12292
  3995.7 293.2 %copy-start.23 = (f32[1024]{0:T(1024)S(1)}, f32[1024]{0:T(1024)}, u32[]{:S(2)}) copy-start(f32[1024]{0:T(1024)} %copy-done.22) | copy-start | bytes 12292
  4016.2 276.1 %copy-start.26 = (f32[1024]{0:T(1024)S(1)}, f32[1024]{0:T(1024)}, u32[]{:S(2)}) copy-start(f32[1024]{0:T(1024)} %get-tuple-element.221) | copy-start | bytes 12292
  4016.2 304.9 %copy-start.24 = (f32[1024]{0:T(1024)S(1)}, f32[1024]{0:T(1024)}, u32[]{:S(2)}) copy-start(f32[1024]{0:T(1024)} %get-tuple-element.293) | copy-start | bytes 12292
  (27 other events, 149.4 us)
Sparse Core Ops, SparseCore 0:
  167.2 59.9 all-gather.8
  825.3 122.4 reduce-scatter.8
  963.5 59.3 all-gather.12
  1024.5 58.2 all-gather.16
  1084.3 635.2 all-gather.14
  1721.1 1061.0 all-gather.18
  2841.1 206.6 reduce-scatter.12
  3050.4 126.1 reduce-scatter.10
  3184.1 58.2 all-gather.20
  3244.5 467.2 all-gather.22
Sparse Core Ops, SparseCore 1:
  538.0 147.7 all-gather.10
  3215.9 795.1 reduce-scatter.22
  4014.6 146.1 reduce-scatter.18
  4163.6 125.1 reduce-scatter.14
  4292.8 710.0 reduce-scatter.20
  5006.8 402.9 reduce-scatter.16
